TPU v7x, 32 devices: a whole 2x2x4 slice. The times are simulated.
32 devices in a mesh: sys: 2 (over y), row: 2 (over x), col: 4 (over z), aux: 2 (over core).
Axes of the slice: x: 2, y: 2, z: 4, core: 2. Of those that a mesh axis runs over, the one named last changes fastest.
Arguments:
- coef_three: bfloat16 [4, 4, 512, 16384], P(('sys', 'row'), 'col', 'aux'), parts along dimension 0, may hold values from -6 to 6
- orbitals: bfloat16 [4, 4, 40, 128], P(('sys', 'row'), 'col'), parts along dimension 0, may hold values from -0.5 to 0.5
- density: bfloat16 [4, 4, 128, 128], P(('sys', 'row'), 'col'), parts along dimension 0, may hold values from -0.5 to 0.5
- pair_mask: int32 [4, 4, 8], P(('sys', 'row'), 'col'), parts along dimension 0, may hold values 0 or 1
Outputs:
- exch_self: float32 [4, 4, 128, 128], P(('sys', 'row'), 'col', 'aux'), parts along dimension 0
- exch_pair: float32 [4, 4, 8, 128, 128], P(('sys', 'row'), 'col', None, 'aux'), parts along dimension 0
- exch_full: float32 [4, 4, 128, 128], P(('sys', 'row'), 'col', 'aux'), parts along dimension 0
There are 2 independent parts, one for each index of `sys`. A program takes and returns all parts, laid end to end along the dimension named above; each array names one. Nothing has to cross between parts.
Inputs may be any that keep to these rules, and one draw needn't show every extreme that they name: `pair_mask`: entries for neighbours outside the grid are drawn like the others and have no effect.
All inputs are finite; a program needn't handle non-finite values. No bound on the sum of `pair_mask` on one device may be relied on, other than what follows from the above.
Results may differ from a plain program's by a relative error of at most 0.0041.
Values may be sent and summed in bfloat16 or wider, within the bound.
A program may use at most 192 MiB of HBM per device.

v0:
```python
import jax
import jax.numpy as jnp
from jax import lax
from jax.sharding import PartitionSpec as P

NB = 128
Q = 512
OCC = 40


def from_behind(value, axis, steps):
    count = lax.axis_size(axis)
    first, last = (max(0, -steps), min(count, count - steps))
    return lax.ppermute(value, axis, [(source, source + steps) for source in range(first, last)])


def contract(left, right):
    return lax.dot_general(
        left, right, (((0,), (0,)), ((), ())), preferred_element_type=jnp.float32
    )


def sideways(block, step):
    return from_behind(block, "col", step)


def returned(block, step):
    return from_behind(block, "col", step)


def local(coef_three, orbitals, density, pair_mask):
    q_local = coef_three.shape[2]
    basis = orbitals.shape[3]
    occupied = orbitals.shape[2]
    coef = coef_three.reshape(q_local * basis, basis)
    value = lax.dot_general(
        orbitals[0, 0], coef, (((1,), (1,)), ((), ())), preferred_element_type=jnp.float32
    )
    half = value.astype(jnp.bfloat16).reshape(occupied * q_local, basis)
    own = contract(half, half)
    dens_half = jnp.dot(coef, density[0, 0], preferred_element_type=jnp.float32).astype(
        jnp.bfloat16
    )
    full_part = lax.dot_general(
        dens_half.reshape(q_local, basis, basis),
        coef.reshape(q_local, basis, basis),
        (((0, 2), (0, 1)), ((), ())),
        preferred_element_type=jnp.float32,
    )
    self_scale = 1.0 / (Q * OCC)
    pair_scale = 1.0 / (Q * OCC) ** 0.5
    full_scale = 1.0 / (Q * NB) ** 0.5
    below = from_behind(half, "row", -1)
    east = sideways(half, -1)
    south_west = sideways(below, 1)
    south_east = sideways(below, -1)
    forward = [
        contract(half, east),
        contract(half, south_west),
        contract(half, below),
        contract(half, south_east),
    ]
    first = jnp.stack([own] + forward + [full_part])
    turned = jnp.swapaxes(jnp.stack(forward), 1, 2)
    mine, theirs = (
        lax.psum_scatter(first, "aux", scatter_dimension=1, tiled=True),
        lax.psum_scatter(turned, "aux", scatter_dimension=1, tiled=True),
    )
    lower = from_behind(theirs[1:], "row", 1)
    pair_part = jnp.stack(
        [
            returned(lower[2], 1),
            lower[1],
            returned(lower[0], -1),
            returned(theirs[0], 1),
            mine[1],
            mine[2],
            mine[3],
            mine[4],
        ]
    )
    self_part = mine[0]
    full_sum = mine[5]
    maskf = pair_mask[0, 0].astype(jnp.float32)
    exch_self = (self_part * self_scale)[None, None]
    exch_pair = (pair_part * pair_scale * maskf[:, None, None])[None, None]
    exch_full = (full_sum * full_scale)[None, None]
    return (exch_self, exch_pair, exch_full)


def solution(mesh):
    in_specs = (
        P(("sys", "row"), "col", "aux", None),
        P(("sys", "row"), "col", None, None),
        P(("sys", "row"), "col", None, None),
        P(("sys", "row"), "col", None),
    )
    out_specs = (
        P(("sys", "row"), "col", "aux", None),
        P(("sys", "row"), "col", None, "aux", None),
        P(("sys", "row"), "col", "aux", None),
    )
    return jax.shard_map(local, mesh=mesh, in_specs=in_specs, out_specs=out_specs, check_vma=False)
```

profile of v0, /device:TPU:0, one launch (start us, length us, event | category | flops | bytes accessed | tf_op | source)
XLA Modules:
  0.0 204.9 jit_solution(17505125538385773471)
XLA Ops:
  7.2 0.0 copy-start
  7.2 0.0 copy-start.2
  7.2 0.0 reduce-scatter.5.cloned.1.call-start
  7.2 13.5 %reshape.118 = bf16[32768,128]{1,0:T(8,128)(2,1)} reshape(bf16[1,1,256,16384]{3,2,1,0:T(8,128)(2,1)} %param.4) | data formatting | bytes 16777216 | tf_op jit(solution)/shard_map/reshape | solution.py:35
  20.7 9.8 %convolution_convert_fusion.1 = bf16[40,32768]{1,0:T(8,128)(2,1)} fusion(bf16[32768,128]{1,0:T(8,128)(2,1)} %reshape.118, bf16[1,1,40,128]{3,2,1,0:T(8,128)(2,1)S(1)} %copy-done.2), kind=kOutput, calls=%fused_computation.1 | convolution fusion | flops 336855040 | bytes 11020288 | tf_op jit(solution)/shard_map/dot_general | solution.py:36
  30.5 3.9 %reshape.119 = bf16[10240,128]{1,0:T(8,128)(2,1)S(1)} reshape(bf16[40,32768]{1,0:T(8,128)(2,1)} %convolution_convert_fusion.1) | data formatting | bytes 5242880 | tf_op jit(solution)/shard_map/reshape | solution.py:39
  34.4 1.3 collective-permute-start.1
  35.7 1.3 collective-permute-start
  37.0 58.6 %collective-permute-done.1 = bf16[10240,128]{1,0:T(8,128)(2,1)S(1)} collective-permute-done((bf16[10240,128]{1,0:T(8,128)(2,1)S(1)}, bf16[10240,128]{1,0:T(8,128)(2,1)S(1)}, u32[]{:S(2)}, u32[]{:S(2)}) %collective-permute-start.1) | collective-permute-done | bytes 2621472 | tf_op jit(solution)/shard_map/ppermute | solution.py:14
  95.6 1.3 collective-permute-start.3
  96.9 5.1 %collective-permute-start.2 = (bf16[10240,128]{1,0:T(8,128)(2,1)S(1)}, bf16[10240,128]{1,0:T(8,128)(2,1)S(1)}, u32[]{:S(2)}, u32[]{:S(2)}) collective-permute-start(bf16[10240,128]{1,0:T(8,128)(2,1)S(1)} %collective-permute-done.1), channel_id=1, source_target_pairs={{0,2},{2,4},{4,6},{1,3},{3,5},{5,7},{8,10},{10,12},{12,14},{9,11},... | collective-permute-start | bytes 7864328 | tf_op jit(solution)/shard_map/ppermute | solution.py:14
  102.0 0.9 fusion
  102.9 9.0 %convolution_convert_fusion = bf16[32768,128]{1,0:T(8,128)(2,1)} fusion(bf16[32768,128]{1,0:T(8,128)(2,1)} %reshape.118, bf16[1,1,128,128]{3,2,1,0:T(8,128)(2,1)S(1)} %copy-done), kind=kOutput, calls=%fused_computation | convolution fusion | flops 1077936128 | bytes 16809984 | tf_op jit(solution)/shard_map/dot_general | solution.py:41
  111.8 1.0 convolution_bitcast_fusion.1
  112.8 0.0 collective-permute-done
  112.8 1.0 convolution_bitcast_fusion.3
  113.8 42.1 %collective-permute-done.3 = bf16[10240,128]{1,0:T(8,128)(2,1)S(1)} collective-permute-done((bf16[10240,128]{1,0:T(8,128)(2,1)S(1)}, bf16[10240,128]{1,0:T(8,128)(2,1)S(1)}, u32[]{:S(2)}, u32[]{:S(2)}) %collective-permute-start.3) | collective-permute-done | bytes 2621472 | tf_op jit(solution)/shard_map/ppermute | solution.py:14
  155.9 1.0 convolution_bitcast_fusion
  156.8 0.0 copy-start.3
  156.9 0.2 collective-permute-done.2
  157.1 1.0 convolution_bitcast_fusion.2
  158.0 0.7 maximum_bitcast_fusion
  158.7 0.0 reduce-scatter.5.cloned.1.call-update
  158.8 0.2 reduce-scatter.3.cloned.1.call-start
  159.0 0.0 copy-done.3
  159.0 9.2 %copy.19 = bf16[32,8,128,128]{3,2,1,0:T(8,128)(2,1)} copy(bf16[32,8,128,128]{3,1,2,0:T(8,128)(2,1)} %bitcast.74) | data formatting | bytes 16777216
  168.2 0.1 copy.11
  168.3 0.1 copy.13
  168.4 0.1 copy.12
  168.5 0.1 copy.14
  168.7 0.0 reduce-scatter.5.cloned.1.call-done
  168.7 0.9 slice.37
  169.6 3.1 %collective-permute-start.4 = (f32[3,64,128]{2,1,0:T(8,128)S(1)}, f32[3,64,128]{2,1,0:T(8,128)S(1)}, u32[]{:S(2)}, u32[]{:S(2)}) collective-permute-start(f32[3,64,128]{2,1,0:T(8,128)S(1)} %slice.37), channel_id=1, source_target_pairs={{0,8},{1,9},{2,10},{3,11},{4,12},{5,13},{6,14},{7,15},{16,24},{17,... | collective-permute-start | bytes 294920 | tf_op jit(solution)/shard_map/ppermute | solution.py:14
  172.7 8.1 %fusion.1 = f32[6,128,128]{2,1,0:T(8,128)S(1)} fusion(f32[6,128,128]{2,1,0:T(8,128)S(1)} %constant_dynamic-update-slice_fusion, bf16[256,128,128]{2,1,0:T(8,128)(2,1)} %bitcast.72, bf16[256,128,128]{2,1,0:T(8,128)(2,1)} %bitcast.73), kind=kOutput, calls=%fused_computation.9 | convolution fusion | flops 1073741824 | bytes 16842752 | tf_op jit(solution)/shard_map/dot_general | solution.py:44
  180.8 0.7 copy-done.1
  181.5 0.0 reduce-scatter.3.cloned.1.call-update
  181.6 0.0 collective-permute-done.4
  181.6 3.4 %collective-permute-start.5 = (f32[64,128]{1,0:T(8,128)S(1)}, f32[64,128]{1,0:T(8,128)S(1)}, u32[]{:S(2)}, u32[]{:S(2)}) collective-permute-start(f32[64,128]{1,0:T(8,128)S(1)} %get-tuple-element.6), channel_id=1, source_target_pairs={{0,2},{2,4},{4,6},{1,3},{3,5},{5,7},{8,10},{10,12},{12,14},{9,11},... | collective-permute-start | bytes 98312 | tf_op jit(solution)/shard_map/ppermute | solution.py:14
  185.0 0.8 slice_bitcast_fusion.1
  185.7 3.4 %collective-permute-start.7 = (f32[64,128]{1,0:T(8,128)S(1)}, f32[64,128]{1,0:T(8,128)S(1)}, u32[]{:S(2)}, u32[]{:S(2)}) collective-permute-start(f32[64,128]{1,0:T(8,128)S(1)} %slice_bitcast_fusion.1), channel_id=1, source_target_pairs={{0,2},{2,4},{4,6},{1,3},{3,5},{5,7},{8,10},{10,12},{12,14},{9,11},... | collective-permute-start | bytes 98312 | tf_op jit(solution)/shard_map/ppermute | solution.py:14
  189.1 1.3 collective-permute-start.6
  190.4 0.0 collective-permute-done.5
  190.5 4.5 %collective-permute-done.6 = f32[64,128]{1,0:T(8,128)S(1)} collective-permute-done((f32[64,128]{1,0:T(8,128)S(1)}, f32[64,128]{1,0:T(8,128)S(1)}, u32[]{:S(2)}, u32[]{:S(2)}) %collective-permute-start.6) | collective-permute-done | bytes 32800 | tf_op jit(solution)/shard_map/ppermute | solution.py:14
  195.0 0.0 collective-permute-done.7
  195.0 0.0 reduce-scatter.3.cloned.1.call-done
  195.0 0.9 fusion.2
  195.9 0.8 broadcast_multiply_fusion
  196.7 1.4 fusion.3
  (13 shorter events, 0.1 us)
Async XLA Ops:
  7.2 95.7 %copy-start = (bf16[1,1,128,128]{3,2,1,0:T(8,128)(2,1)S(1)}, bf16[1,1,128,128]{3,2,1,0:T(8,128)(2,1)}, u32[]{:S(2)}) copy-start(bf16[1,1,128,128]{3,2,1,0:T(8,128)(2,1)} %param.6) | copy-start | bytes 98308
  7.2 13.6 %copy-start.2 = (bf16[1,1,40,128]{3,2,1,0:T(8,128)(2,1)S(1)}, bf16[1,1,40,128]{3,2,1,0:T(8,128)(2,1)}, u32[]{:S(2)}) copy-start(bf16[1,1,40,128]{3,2,1,0:T(8,128)(2,1)} %param.5) | copy-start | bytes 30724
  7.2 161.5 %reduce-scatter.5.cloned.1.call-start = ((), (), s32[]{:S(2)}) async-start(), calls=%async_computation.3 | async-start | bytes 393216 | tf_op jit(solution)/shard_map/reduce_scatter | solution.py:67
  34.4 61.2 %collective-permute-start.1 = (bf16[10240,128]{1,0:T(8,128)(2,1)S(1)}, bf16[10240,128]{1,0:T(8,128)(2,1)S(1)}, u32[]{:S(2)}, u32[]{:S(2)}) collective-permute-start(bf16[10240,128]{1,0:T(8,128)(2,1)S(1)} %reshape.119), channel_id=1, source_target_pairs={{8,0},{9,1},{10,2},{11,3},{12,4},{13,5},{14,6},{15,7},{24,16},{25,... | collective-permute-start | bytes 7864328 | tf_op jit(solution)/shard_map/ppermute | solution.py:14
  35.7 77.1 %collective-permute-start = (bf16[10240,128]{1,0:T(8,128)(2,1)S(1)}, bf16[10240,128]{1,0:T(8,128)(2,1)S(1)}, u32[]{:S(2)}, u32[]{:S(2)}) collective-permute-start(bf16[10240,128]{1,0:T(8,128)(2,1)S(1)} %reshape.119), channel_id=1, source_target_pairs={{2,0},{4,2},{6,4},{3,1},{5,3},{7,5},{10,8},{12,10},{14,12},{11,9},... | collective-permute-start | bytes 7864328 | tf_op jit(solution)/shard_map/ppermute | solution.py:14
  95.6 60.3 %collective-permute-start.3 = (bf16[10240,128]{1,0:T(8,128)(2,1)S(1)}, bf16[10240,128]{1,0:T(8,128)(2,1)S(1)}, u32[]{:S(2)}, u32[]{:S(2)}) collective-permute-start(bf16[10240,128]{1,0:T(8,128)(2,1)S(1)} %collective-permute-done.1), channel_id=1, source_target_pairs={{2,0},{4,2},{6,4},{3,1},{5,3},{7,5},{10,8},{12,10},{14,12},{11,9},... | collective-permute-start | bytes 7864328 | tf_op jit(solution)/shard_map/ppermute | solution.py:14
  96.9 60.2 %collective-permute-start.2 = (bf16[10240,128]{1,0:T(8,128)(2,1)S(1)}, bf16[10240,128]{1,0:T(8,128)(2,1)S(1)}, u32[]{:S(2)}, u32[]{:S(2)}) collective-permute-start(bf16[10240,128]{1,0:T(8,128)(2,1)S(1)} %collective-permute-done.1), channel_id=1, source_target_pairs={{0,2},{2,4},{4,6},{1,3},{3,5},{5,7},{8,10},{10,12},{12,14},{9,11},... | collective-permute-start | bytes 7864328 | tf_op jit(solution)/shard_map/ppermute | solution.py:14
  156.8 2.2 %copy-start.3 = (s32[1,1,8]{2,1,0:T(1,128)S(1)}, s32[1,1,8]{2,1,0:T(1,128)}, u32[]{:S(2)}) copy-start(s32[1,1,8]{2,1,0:T(1,128)} %param.7) | copy-start | bytes 100
  158.8 36.2 %reduce-scatter.3.cloned.1.call-start = ((), (), s32[]{:S(2)}) async-start(), calls=%async_computation.2 | async-start | bytes 589824 | tf_op jit(solution)/shard_map/reduce_scatter | solution.py:66
  169.6 12.0 %collective-permute-start.4 = (f32[3,64,128]{2,1,0:T(8,128)S(1)}, f32[3,64,128]{2,1,0:T(8,128)S(1)}, u32[]{:S(2)}, u32[]{:S(2)}) collective-permute-start(f32[3,64,128]{2,1,0:T(8,128)S(1)} %slice.37), channel_id=1, source_target_pairs={{0,8},{1,9},{2,10},{3,11},{4,12},{5,13},{6,14},{7,15},{16,24},{17,... | collective-permute-start | bytes 294920 | tf_op jit(solution)/shard_map/ppermute | solution.py:14
  180.8 0.7 copy-start.1
  181.6 8.9 %collective-permute-start.5 = (f32[64,128]{1,0:T(8,128)S(1)}, f32[64,128]{1,0:T(8,128)S(1)}, u32[]{:S(2)}, u32[]{:S(2)}) collective-permute-start(f32[64,128]{1,0:T(8,128)S(1)} %get-tuple-element.6), channel_id=1, source_target_pairs={{0,2},{2,4},{4,6},{1,3},{3,5},{5,7},{8,10},{10,12},{12,14},{9,11},... | collective-permute-start | bytes 98312 | tf_op jit(solution)/shard_map/ppermute | solution.py:14
  185.7 9.2 %collective-permute-start.7 = (f32[64,128]{1,0:T(8,128)S(1)}, f32[64,128]{1,0:T(8,128)S(1)}, u32[]{:S(2)}, u32[]{:S(2)}) collective-permute-start(f32[64,128]{1,0:T(8,128)S(1)} %slice_bitcast_fusion.1), channel_id=1, source_target_pairs={{0,2},{2,4},{4,6},{1,3},{3,5},{5,7},{8,10},{10,12},{12,14},{9,11},... | collective-permute-start | bytes 98312 | tf_op jit(solution)/shard_map/ppermute | solution.py:14
  189.1 5.8 %collective-permute-start.6 = (f32[64,128]{1,0:T(8,128)S(1)}, f32[64,128]{1,0:T(8,128)S(1)}, u32[]{:S(2)}, u32[]{:S(2)}) collective-permute-start(f32[64,128]{1,0:T(8,128)S(1)} %get-tuple-element.5), channel_id=1, source_target_pairs={{2,0},{4,2},{6,4},{3,1},{5,3},{7,5},{10,8},{12,10},{14,12},{11,9},... | collective-permute-start | bytes 98312 | tf_op jit(solution)/shard_map/ppermute | solution.py:14
Sparse Core Ops, SparseCore 0:
  158.9 9.2 reduce-scatter.4
  181.7 7.8 reduce-scatter.2
where the time goes:
time: 206 us; the launch traced here: 205 us
  waiting for transfers between devices  105 us (51%)
  matrix products  31.6 us (15%)
  local copies, waits for them, and re-layouts  30.3 us (15%)
  starting transfers between devices  20.4 us (10%)
  between operations  14.3 us (7%)
  other arithmetic  2.92 us (1%)
    ppermute x8, waiting for transfers between devices, from_behind(): lax.ppermute(value, axis, [(source, source + steps) for source in range(f...  105 us
    ppermute x8, starting transfers between devices, from_behind(): lax.ppermute(value, axis, [(source, source + steps) for source in range(f...  20.1 us
    reshape x1, local copies, waits for them, and re-layouts, local(): coef = coef_three.reshape(q_local * basis, basis)  13.5 us
    unnamed x17, local copies, waits for them, and re-layouts  9.99 us
    dot_general x1, matrix products, local(): lax.dot_general(orbitals[0, 0], coef, (((1,), (1,)), ((), ())), preferred...  9.8 us
    dot_general x1, matrix products, local(): jnp.dot(coef, density[0, 0], preferred_element_type=jnp.float32)  8.95 us
    dot_general x1, matrix products, local(): lax.dot_general(dens_half.reshape(q_local, basis, basis), coef.reshape(q_...  8.1 us
    dot_general x5, matrix products, contract(): lax.dot_general(left, right, (((0,), (0,)), ((), ())), preferred_element_...  4.72 us
  transfers between devices with their start and end apart: 10, of which 4 were waited for; matrix products, arithmetic and copies ran while one was open for 15% of the time, Pallas kernels for 0%

commit v1 on v0

v1 whole, which is shorter than its diff:
```python
import functools

import jax
import jax.numpy as jnp
from jax import lax
from jax.experimental import pallas as pl
from jax.experimental.pallas import tpu as pltpu
from jax.sharding import PartitionSpec as P

MESH = pl.DeviceIdType.MESH
LEFT, RIGHT, UP, DOWN, OWN = range(5)
OPPOSITE = (RIGHT, LEFT, DOWN, UP)
NAMES = (
    (OWN, LEFT), (OWN, RIGHT), (OWN, UP), (OWN, DOWN),
    (LEFT, UP), (LEFT, DOWN), (RIGHT, UP), (RIGHT, DOWN),
)
PLAN = (
    (((RIGHT, None), (UP, None), (DOWN, None)),
     ((OWN, LEFT), (OWN, DOWN), (LEFT, DOWN), (LEFT, UP))),
    (((LEFT, None), (UP, None), (DOWN, None)),
     ((OWN, RIGHT), (OWN, DOWN), (RIGHT, DOWN), (RIGHT, UP))),
    (((RIGHT, None), (LEFT, DOWN), (UP, None)),
     ((OWN, LEFT), (OWN, DOWN), (LEFT, DOWN), (RIGHT, DOWN))),
    (((RIGHT, UP), (LEFT, None), (DOWN, None)),
     ((OWN, RIGHT), (OWN, UP), (LEFT, UP), (RIGHT, UP))),
    (((RIGHT, DOWN), (LEFT, None), (UP, None)),
     ((OWN, RIGHT), (OWN, DOWN), (LEFT, DOWN), (RIGHT, DOWN))),
    (((RIGHT, None), (LEFT, UP), (DOWN, None)),
     ((OWN, LEFT), (OWN, UP), (LEFT, UP), (RIGHT, UP))),
)


def row_dot(left, right):
    return lax.dot_general(
        left, right, (((1,), (1,)), ((), ())), preferred_element_type=jnp.float32
    )


def cut(total):
    parts = len(PLAN)
    ends = [(total * i) // parts for i in range(parts + 1)]
    return list(zip(ends[:-1], ends[1:]))


def turn_block(stage, count, rows, store):
    lanes = stage.shape[2]
    for part in range(stage.shape[0]):
        for o in range(rows):
            piece = stage[part, pl.ds(o, count, stride=rows), :]
            store(o, slice(part * lanes, (part + 1) * lanes), piece.astype(jnp.bfloat16))


def half_kernel(orb_ref, coef_ref, out_ref, stage):
    occ, basis = orb_ref.shape
    block = out_ref.shape[1]
    lanes = stage.shape[2]
    orb = orb_ref[...]
    for m in range(block):
        value = row_dot(orb, coef_ref[:, m * basis:(m + 1) * basis])
        for part in range(stage.shape[0]):
            stage[part, m * occ:(m + 1) * occ, :] = value[:, part * lanes:(part + 1) * lanes]

    def store(o, columns, piece):
        out_ref[o, :, columns] = piece

    turn_block(stage, block, occ, store)


def half_transform(coef, orbitals):
    q_local, width = coef.shape
    occ, basis = orbitals.shape
    block = 16
    lanes = 128
    return pl.pallas_call(
        half_kernel,
        grid=(width // basis // block,),
        out_shape=jax.ShapeDtypeStruct((occ, width // basis, q_local), jnp.bfloat16),
        in_specs=[
            pl.BlockSpec((occ, basis), lambda i: (0, 0)),
            pl.BlockSpec((q_local, block * basis), lambda i: (0, i)),
        ],
        out_specs=pl.BlockSpec((occ, block, q_local), lambda i: (0, i, 0)),
        scratch_shapes=[pltpu.VMEM((q_local // lanes, block * occ, lanes), jnp.float32)],
        compiler_params=pltpu.CompilerParams(vmem_limit_bytes=24 << 20),
        name="half_transform",
    )(orbitals, coef)


def exchange_kernel(
    rows, cols, scales, half_hbm, coef_hbm, dens_ref, mask_ref,
    self_ref, pair_ref, full_ref,
    blocks, coef, stage, dens_half, acc, outbox, inbox, local, final, aux_local, aux_final,
    load_sem, send_sem, recv_sem, box_send, box_recv, aux_send, aux_recv,
):
    occ, basis, q_local = half_hbm.shape
    r, c, a = lax.axis_index("row"), lax.axis_index("col"), lax.axis_index("aux")
    has = (c > 0, c < cols - 1, r > 0, r < rows - 1)
    where = ({"col": c - 1}, {"col": c + 1}, {"row": r - 1}, {"row": r + 1})
    partner = {"aux": 1 - a}
    slices = cut(occ)

    load_coef = pltpu.make_async_copy(coef_hbm, coef, load_sem.at[0])
    load_half = pltpu.make_async_copy(half_hbm, blocks.at[OWN], load_sem.at[1])
    load_half.start()
    load_coef.start()

    barrier = pltpu.get_barrier_semaphore()
    pl.semaphore_signal(barrier, inc=1, device_id=partner, device_id_type=MESH)
    for side in range(4):
        @pl.when(has[side])
        def _(side=side):
            pl.semaphore_signal(barrier, inc=1, device_id=where[side], device_id_type=MESH)
    expected = 1 + sum(flag.astype(jnp.int32) for flag in has)
    pl.semaphore_wait(barrier, expected)

    def transfer(index, side):
        start, end = slices[index]
        return pltpu.make_async_remote_copy(
            src_ref=half_hbm.at[pl.ds(start, end - start)],
            dst_ref=blocks.at[OPPOSITE[side], pl.ds(start, end - start)],
            send_sem=send_sem.at[side, index],
            recv_sem=recv_sem.at[OPPOSITE[side], index],
            device_id=where[side],
            device_id_type=MESH,
        )

    def arrival(index, side):
        start, end = slices[index]
        return pltpu.make_async_remote_copy(
            src_ref=half_hbm.at[pl.ds(start, end - start)],
            dst_ref=blocks.at[side, pl.ds(start, end - start)],
            send_sem=send_sem.at[side, index],
            recv_sem=recv_sem.at[side, index],
            device_id=where[side],
            device_id_type=MESH,
        )

    def both(first, second):
        return first if second is None else jnp.logical_and(first, second)

    def flag_of(condition):
        return None if condition is None else has[condition]

    for index, (sends, _) in enumerate(PLAN):
        for side, condition in sends:
            @pl.when(both(has[side], flag_of(condition)))
            def _(index=index, side=side):
                transfer(index, side).start()

    for index in range(len(NAMES)):
        acc[index] = jnp.zeros((basis, basis), jnp.float32)
    for side in range(4):
        @pl.when(jnp.logical_not(has[side]))
        def _(side=side):
            inbox[side] = jnp.zeros(inbox.shape[1:], jnp.float32)

    def product(first, second, start, end):
        left = jnp.concatenate([blocks[first, o] for o in range(start, end)], axis=1)
        right = jnp.concatenate([blocks[second, o] for o in range(start, end)], axis=1)
        return row_dot(left, right)

    load_half.wait()
    load_coef.wait()

    dens_turned = dens_ref[...].astype(jnp.float32).T.astype(jnp.bfloat16)
    lanes = stage.shape[2]
    block = stage.shape[1] // basis

    @pl.loop(0, basis // block)
    def _(step):
        @pl.loop(0, block)
        def _(m):
            at = pl.multiple_of((step * block + m) * basis, basis)
            value = row_dot(dens_turned, coef[:, pl.ds(at, basis)])
            to = pl.multiple_of(m * basis, basis)
            for part in range(stage.shape[0]):
                stage[part, pl.ds(to, basis), :] = value[:, part * lanes:(part + 1) * lanes]

        first = pl.multiple_of(step * block, block)

        @pl.loop(0, basis // 8)
        def _(group):
            for k in range(8):
                s = group * 8 + k
                for part in range(stage.shape[0]):
                    piece = stage[part, pl.ds(s, block, stride=basis), :]
                    dens_half[s, pl.ds(first, block), part * lanes:(part + 1) * lanes] = (
                        piece.astype(jnp.bfloat16)
                    )

    local[0] = jnp.zeros((basis, basis), jnp.float32)
    local[1] = jnp.zeros((basis, basis), jnp.float32)

    @pl.loop(0, basis // 8)
    def _(group):
        left = jnp.concatenate([dens_half[group * 8 + k] for k in range(8)], axis=1)
        right = jnp.concatenate(
            [
                coef[:, pl.ds(pl.multiple_of((group * 8 + k) * basis, basis), basis)]
                for k in range(8)
            ],
            axis=0,
        )
        local[1] += jnp.dot(left, right, preferred_element_type=jnp.float32)

    @pl.loop(0, occ // 8)
    def _(group):
        mine = jnp.concatenate([blocks[OWN, group * 8 + k] for k in range(8)], axis=1)
        local[0] += row_dot(mine, mine)

    rows_out = basis // 2
    theirs = pl.ds(pl.multiple_of((1 - a) * rows_out, rows_out), rows_out)
    ours = pl.ds(pl.multiple_of(a * rows_out, rows_out), rows_out)

    def to_partner(source, target, which):
        return pltpu.make_async_remote_copy(
            src_ref=source.at[:, theirs, :],
            dst_ref=target,
            send_sem=aux_send.at[which],
            recv_sem=aux_recv.at[which],
            device_id=partner,
            device_id_type=MESH,
        )

    swap_local = to_partner(local, aux_local, 0)
    swap_local.start()

    for index, (sends, products) in enumerate(PLAN):
        start, end = slices[index]
        for side, condition in sends:
            source = OPPOSITE[side]

            @pl.when(both(has[source], flag_of(condition)))
            def _(index=index, source=source):
                arrival(index, source).wait_recv()

        for first, second in products:
            there = has[second] if first == OWN else jnp.logical_and(has[first], has[second])

            @pl.when(there)
            def _(first=first, second=second, start=start, end=end):
                acc[NAMES.index((first, second))] += product(first, second, start, end)

    def post(side):
        return pltpu.make_async_remote_copy(
            src_ref=outbox.at[side],
            dst_ref=inbox.at[OPPOSITE[side]],
            send_sem=box_send.at[side],
            recv_sem=box_recv.at[OPPOSITE[side]],
            device_id=where[side],
            device_id_type=MESH,
        )

    def collect(side):
        return pltpu.make_async_remote_copy(
            src_ref=outbox.at[side],
            dst_ref=inbox.at[side],
            send_sem=box_send.at[side],
            recv_sem=box_recv.at[side],
            device_id=where[side],
            device_id_type=MESH,
        )

    def value(first, second):
        return acc[NAMES.index((first, second))]

    outbox[LEFT, 0] = value(OWN, LEFT).T
    outbox[LEFT, 1] = value(LEFT, UP)
    outbox[LEFT, 2] = value(LEFT, DOWN)
    outbox[RIGHT, 0] = value(OWN, RIGHT).T
    outbox[RIGHT, 1] = value(RIGHT, UP)
    outbox[RIGHT, 2] = value(RIGHT, DOWN)
    outbox[UP, 0] = value(OWN, UP).T
    outbox[UP, 1] = value(LEFT, UP).T
    outbox[UP, 2] = value(RIGHT, UP).T
    outbox[DOWN, 0] = value(OWN, DOWN).T
    outbox[DOWN, 1] = value(LEFT, DOWN).T
    outbox[DOWN, 2] = value(RIGHT, DOWN).T
    for side in range(4):
        @pl.when(has[side])
        def _(side=side):
            post(side).start()
    for side in range(4):
        @pl.when(has[side])
        def _(side=side):
            collect(side).wait_recv()

    final[0] = inbox[LEFT, 1] + inbox[UP, 1]
    final[1] = value(OWN, UP) + inbox[UP, 0]
    final[2] = inbox[RIGHT, 1] + inbox[UP, 2]
    final[3] = value(OWN, LEFT) + inbox[LEFT, 0]
    final[4] = value(OWN, RIGHT) + inbox[RIGHT, 0]
    final[5] = inbox[LEFT, 2] + inbox[DOWN, 1]
    final[6] = value(OWN, DOWN) + inbox[DOWN, 0]
    final[7] = inbox[RIGHT, 2] + inbox[DOWN, 2]
    swap_final = to_partner(final, aux_final, 1)
    swap_final.start()

    self_scale, pair_scale, full_scale = scales
    swap_local.wait_recv()
    self_ref[0, 0] = (local[0, ours, :] + aux_local[0]) * self_scale
    full_ref[0, 0] = (local[1, ours, :] + aux_local[1]) * full_scale
    swap_final.wait_recv()
    for d in range(8):
        factor = mask_ref[d].astype(jnp.float32)
        pair_ref[0, 0, d] = (final[d, ours, :] + aux_final[d]) * pair_scale * factor

    swap_local.wait_send()
    swap_final.wait_send()
    for side in range(4):
        @pl.when(has[side])
        def _(side=side):
            post(side).wait_send()
    for index, (sends, _) in enumerate(PLAN):
        for side, condition in sends:
            @pl.when(both(has[side], flag_of(condition)))
            def _(index=index, side=side):
                transfer(index, side).wait_send()


def local_step(rows, cols, aux, coef_three, orbitals, density, pair_mask):
    q_local, width = coef_three.shape[2:]
    occ, basis = orbitals.shape[2:]
    coef = coef_three[0, 0]
    q_total = q_local * aux
    scales = (
        1.0 / (q_total * occ), 1.0 / (q_total * occ) ** 0.5, 1.0 / (q_total * basis) ** 0.5
    )
    half = half_transform(coef, orbitals[0, 0])
    rows_out = basis // aux
    lanes = 128
    f32 = jnp.float32
    dma = pltpu.SemaphoreType.DMA
    vmem = pl.BlockSpec(memory_space=pltpu.VMEM)
    return pl.pallas_call(
        functools.partial(exchange_kernel, rows, cols, scales),
        out_shape=(
            jax.ShapeDtypeStruct((1, 1, rows_out, basis), f32),
            jax.ShapeDtypeStruct((1, 1, 8, rows_out, basis), f32),
            jax.ShapeDtypeStruct((1, 1, rows_out, basis), f32),
        ),
        in_specs=[
            pl.BlockSpec(memory_space=pl.ANY),
            pl.BlockSpec(memory_space=pl.ANY),
            vmem,
            pl.BlockSpec(memory_space=pltpu.SMEM),
        ],
        out_specs=(vmem, vmem, vmem),
        scratch_shapes=[
            pltpu.VMEM((5, occ, basis, q_local), jnp.bfloat16),
            pltpu.VMEM((q_local, width), jnp.bfloat16),
            pltpu.VMEM((q_local // lanes, 16 * basis, lanes), f32),
            pltpu.VMEM((basis, basis, q_local), jnp.bfloat16),
            pltpu.VMEM((8, basis, basis), f32),
            pltpu.VMEM((4, 3, basis, basis), f32),
            pltpu.VMEM((4, 3, basis, basis), f32),
            pltpu.VMEM((2, basis, basis), f32),
            pltpu.VMEM((8, basis, basis), f32),
            pltpu.VMEM((2, rows_out, basis), f32),
            pltpu.VMEM((8, rows_out, basis), f32),
            dma((2,)),
            dma((4, len(PLAN))),
            dma((4, len(PLAN))),
            dma((4,)),
            dma((4,)),
            dma((2,)),
            dma((2,)),
        ],
        compiler_params=pltpu.CompilerParams(
            collective_id=0, has_side_effects=True, vmem_limit_bytes=56 << 20
        ),
        name="exchange",
    )(half, coef, density[0, 0], pair_mask[0, 0])


def solution(mesh):
    in_specs = (
        P(("sys", "row"), "col", "aux", None),
        P(("sys", "row"), "col", None, None),
        P(("sys", "row"), "col", None, None),
        P(("sys", "row"), "col", None),
    )
    out_specs = (
        P(("sys", "row"), "col", "aux", None),
        P(("sys", "row"), "col", None, "aux", None),
        P(("sys", "row"), "col", "aux", None),
    )
    body = functools.partial(local_step, mesh.shape["row"], mesh.shape["col"], mesh.shape["aux"])
    return jax.shard_map(body, mesh=mesh, in_specs=in_specs, out_specs=out_specs, check_vma=False)
```

time: 206 us -> 75.9 us (0.37)
  waiting for transfers between devices: 105 us -> 0 us
  Pallas kernels: 0 us -> 64.8 us
  matrix products: 31.6 us -> 0 us
  starting transfers between devices: 20.4 us -> 0 us
  local copies, waits for them, and re-layouts: 30.3 us -> 9.99 us
  between operations: 14.3 us -> 0.66 us
  other arithmetic: 2.92 us -> 0 us
    ppermute x8 -> x0, waiting for transfers between devices: 105 us -> none  [from_behind(): lax.ppermute(value, axis, [(source, source + steps) for source in range(f...]
    pallas_call x0 -> x2, Pallas kernels: none -> 64.8 us  [the longest x1 59.7 us: local_step(): pl.pallas_call(functools.partial(exchange_kernel, rows, cols, scales), ou...]
    dot_general x8 -> x0, matrix products: 31.6 us -> none  [the longest x1 9.8 us: local(): lax.dot_general(orbitals[0, 0], coef, (((1,), (1,)), ((), ())), preferred...]
    ppermute x8 -> x0, starting transfers between devices: 20.1 us -> none  [from_behind(): lax.ppermute(value, axis, [(source, source + steps) for source in range(f...]
    reshape x2 -> x0, local copies, waits for them, and re-layouts: 17.4 us -> none  [the longest x1 13.5 us: local(): coef = coef_three.reshape(q_local * basis, basis)]
    mul x3 -> x0, other arithmetic: 2.2 us -> none  [the longest x1 1.4 us: local(): exch_full = (full_sum * full_scale)[None, None]]
    unnamed x17 -> x9, local copies, waits for them, and re-layouts: 9.99 us -> 9.99 us
  transfers between devices with their start and end apart: 10 -> 0, of which waited for: 4 -> 0; matrix products, arithmetic and copies ran while one was open for 15% -> 0% of each run, Pallas kernels for 0% -> 0%
where the time goes in v1:
time: 75.9 us; the launch traced here: 75.5 us
  Pallas kernels  64.8 us (85%)
  local copies, waits for them, and re-layouts  9.99 us (13%)
    pallas_call x1, Pallas kernels, local_step(): pl.pallas_call(functools.partial(exchange_kernel, rows, cols, scales), ou...  59.7 us
    unnamed x9, local copies, waits for them, and re-layouts  9.99 us
    pallas_call x1, Pallas kernels, half_transform(): pl.pallas_call(half_kernel, grid=(width // basis // block,), out_shape=ja...  5.1 us

profile of v1, /device:TPU:0, one launch (start us, length us, event | category | flops | bytes accessed | tf_op | source)
XLA Modules:
  0.0 75.5 jit_solution(12121093652594798356)
XLA Ops:
  0.6 0.0 copy-start
  0.6 3.4 %copy-done = bf16[1,1,256,16384]{3,2,1,0:T(8,128)(2,1)S(1)} copy-done((bf16[1,1,256,16384]{3,2,1,0:T(8,128)(2,1)S(1)}, bf16[1,1,256,16384]{3,2,1,0:T(8,128)(2,1)}, u32[]{:S(2)}) %copy-start) | copy-done | bytes 8388632
  4.0 0.0 copy-start.2
  4.0 0.7 copy-done.2
  4.7 5.1 %half_transform.1.half_hbm = bf16[40,128,256]{2,1,0:T(8,128)(2,1)S(1)} custom-call(bf16[40,128]{1,0:T(8,128)(2,1)S(1)} %bitcast.6, bf16[256,16384]{1,0:T(8,128)(2,1)S(1)} %bitcast.5), custom_call_target="tpu_custom_call" | custom-call | tf_op jit(solution)/shard_map/half_transform/pallas_call | solution.py:74
  9.8 0.0 copy-start.1
  9.8 1.5 %copy-done.1 = bf16[40,128,256]{2,1,0:T(8,128)(2,1)} copy-done((bf16[40,128,256]{2,1,0:T(8,128)(2,1)}, bf16[40,128,256]{2,1,0:T(8,128)(2,1)S(1)}, u32[]{:S(2)}) %copy-start.1) | copy-done | bytes 2621464
  11.3 59.7 %exchange.1 = (f32[1,1,64,128]{3,2,1,0:T(8,128)}, f32[1,1,8,64,128]{4,3,2,1,0:T(8,128)}, f32[1,1,64,128]{3,2,1,0:T(8,128)}) custom-call(bf16[40,128,256]{2,1,0:T(8,128)(2,1)} %copy-done.1, bf16[256,16384]{1,0:T(8,128)(2,1)} %bitcast.4, bf16[128,128]{1,0:T(8,128)(2,1)} %bitcast.7, s32[8]{0:T(128)} %bitcast.8), custom_call_target="tpu_custom_call" | custom-call | tf_op jit(solution)/shard_map/exchange/pallas_call | solution.py:335
  71.1 1.4 %copy.10 = f32[1,1,64,128]{3,2,1,0:T(8,128)} copy(f32[1,1,64,128]{3,2,1,0:T(8,128)} %get-tuple-element.6) | data formatting | bytes 65536
  72.4 1.7 %copy.11 = f32[1,1,8,64,128]{4,3,2,1,0:T(8,128)} copy(f32[1,1,8,64,128]{4,3,2,1,0:T(8,128)} %get-tuple-element.7) | data formatting | bytes 524288
  74.1 1.4 %copy.12 = f32[1,1,64,128]{3,2,1,0:T(8,128)} copy(f32[1,1,64,128]{3,2,1,0:T(8,128)} %get-tuple-element.8) | data formatting | bytes 65536
Async XLA Ops:
  0.6 3.4 %copy-start = (bf16[1,1,256,16384]{3,2,1,0:T(8,128)(2,1)S(1)}, bf16[1,1,256,16384]{3,2,1,0:T(8,128)(2,1)}, u32[]{:S(2)}) copy-start(bf16[1,1,256,16384]{3,2,1,0:T(8,128)(2,1)} %param.4) | copy-start | bytes 25165828
  4.0 0.7 copy-start.2
  9.8 1.5 %copy-start.1 = (bf16[40,128,256]{2,1,0:T(8,128)(2,1)}, bf16[40,128,256]{2,1,0:T(8,128)(2,1)S(1)}, u32[]{:S(2)}) copy-start(bf16[40,128,256]{2,1,0:T(8,128)(2,1)S(1)} %half_transform.1.half_hbm) | copy-start | bytes 7864324

commit v2 on v1

--- a/solution.py
+++ b/solution.py
@@ -42,67 +42,33 @@
     return list(zip(ends[:-1], ends[1:]))
 
 
-def turn_block(stage, count, rows, store):
-    lanes = stage.shape[2]
-    for part in range(stage.shape[0]):
-        for o in range(rows):
-            piece = stage[part, pl.ds(o, count, stride=rows), :]
-            store(o, slice(part * lanes, (part + 1) * lanes), piece.astype(jnp.bfloat16))
-
-
-def half_kernel(orb_ref, coef_ref, out_ref, stage):
-    occ, basis = orb_ref.shape
-    block = out_ref.shape[1]
-    lanes = stage.shape[2]
-    orb = orb_ref[...]
-    for m in range(block):
-        value = row_dot(orb, coef_ref[:, m * basis:(m + 1) * basis])
-        for part in range(stage.shape[0]):
-            stage[part, m * occ:(m + 1) * occ, :] = value[:, part * lanes:(part + 1) * lanes]
-
-    def store(o, columns, piece):
-        out_ref[o, :, columns] = piece
-
-    turn_block(stage, block, occ, store)
-
-
-def half_transform(coef, orbitals):
-    q_local, width = coef.shape
-    occ, basis = orbitals.shape
-    block = 16
-    lanes = 128
-    return pl.pallas_call(
-        half_kernel,
-        grid=(width // basis // block,),
-        out_shape=jax.ShapeDtypeStruct((occ, width // basis, q_local), jnp.bfloat16),
-        in_specs=[
-            pl.BlockSpec((occ, basis), lambda i: (0, 0)),
-            pl.BlockSpec((q_local, block * basis), lambda i: (0, i)),
-        ],
-        out_specs=pl.BlockSpec((occ, block, q_local), lambda i: (0, i, 0)),
-        scratch_shapes=[pltpu.VMEM((q_local // lanes, block * occ, lanes), jnp.float32)],
-        compiler_params=pltpu.CompilerParams(vmem_limit_bytes=24 << 20),
-        name="half_transform",
-    )(orbitals, coef)
-
-
 def exchange_kernel(
-    rows, cols, scales, half_hbm, coef_hbm, dens_ref, mask_ref,
-    self_ref, pair_ref, full_ref,
+    rows, cols, coef_hbm, orb_ref, dens_ref, out_ref,
     blocks, coef, stage, dens_half, acc, outbox, inbox, local, final, aux_local, aux_final,
     load_sem, send_sem, recv_sem, box_send, box_recv, aux_send, aux_recv,
 ):
-    occ, basis, q_local = half_hbm.shape
+    occ, basis = orb_ref.shape
+    q_local = coef_hbm.shape[0]
     r, c, a = lax.axis_index("row"), lax.axis_index("col"), lax.axis_index("aux")
     has = (c > 0, c < cols - 1, r > 0, r < rows - 1)
     where = ({"col": c - 1}, {"col": c + 1}, {"row": r - 1}, {"row": r + 1})
     partner = {"aux": 1 - a}
     slices = cut(occ)
 
-    load_coef = pltpu.make_async_copy(coef_hbm, coef, load_sem.at[0])
-    load_half = pltpu.make_async_copy(half_hbm, blocks.at[OWN], load_sem.at[1])
-    load_half.start()
-    load_coef.start()
+    parts, _, lanes = stage.shape
+    block = stage.shape[1] // basis
+    steps = basis // block
+
+    def load(part, step):
+        to = pl.multiple_of(step * (block * basis), block * basis)
+        piece = (pl.ds(part * lanes, lanes), pl.ds(to, block * basis))
+        return pltpu.make_async_copy(
+            coef_hbm.at[piece], coef.at[piece], load_sem.at[part, step]
+        )
+
+    for part in range(parts):
+        for step in range(steps):
+            load(part, step).start()
 
     barrier = pltpu.get_barrier_semaphore()
     pl.semaphore_signal(barrier, inc=1, device_id=partner, device_id_type=MESH)
@@ -113,27 +79,23 @@
     expected = 1 + sum(flag.astype(jnp.int32) for flag in has)
     pl.semaphore_wait(barrier, expected)
 
-    def transfer(index, side):
+    def copy(index, part, side, slot):
         start, end = slices[index]
+        piece = (pl.ds(start, end - start), slice(None), pl.ds(part * lanes, lanes))
         return pltpu.make_async_remote_copy(
-            src_ref=half_hbm.at[pl.ds(start, end - start)],
-            dst_ref=blocks.at[OPPOSITE[side], pl.ds(start, end - start)],
-            send_sem=send_sem.at[side, index],
-            recv_sem=recv_sem.at[OPPOSITE[side], index],
+            src_ref=blocks.at[(OWN,) + piece],
+            dst_ref=blocks.at[(slot,) + piece],
+            send_sem=send_sem.at[side, index, part],
+            recv_sem=recv_sem.at[slot, index, part],
             device_id=where[side],
             device_id_type=MESH,
         )
 
-    def arrival(index, side):
-        start, end = slices[index]
-        return pltpu.make_async_remote_copy(
-            src_ref=half_hbm.at[pl.ds(start, end - start)],
-            dst_ref=blocks.at[side, pl.ds(start, end - start)],
-            send_sem=send_sem.at[side, index],
-            recv_sem=recv_sem.at[side, index],
-            device_id=where[side],
-            device_id_type=MESH,
-        )
+    def transfer(index, part, side):
+        return copy(index, part, side, OPPOSITE[side])
+
+    def arrival(index, part, side):
+        return copy(index, part, side, side)
 
     def both(first, second):
         return first if second is None else jnp.logical_and(first, second)
@@ -141,11 +103,28 @@
     def flag_of(condition):
         return None if condition is None else has[condition]
 
-    for index, (sends, _) in enumerate(PLAN):
-        for side, condition in sends:
-            @pl.when(both(has[side], flag_of(condition)))
-            def _(index=index, side=side):
-                transfer(index, side).start()
+    orb = orb_ref[...]
+    for part in range(parts):
+        @pl.loop(0, steps)
+        def _(step, part=part):
+            load(part, step).wait()
+            for m in range(block):
+                at = pl.multiple_of((step * block + m) * basis, basis)
+                stage[part, m * occ:(m + 1) * occ, :] = row_dot(
+                    orb, coef[part * lanes:(part + 1) * lanes, pl.ds(at, basis)]
+                )
+            first = pl.multiple_of(step * block, block)
+            for o in range(occ):
+                piece = stage[part, pl.ds(o, block, stride=occ), :]
+                blocks[OWN, o, pl.ds(first, block), part * lanes:(part + 1) * lanes] = (
+                    piece.astype(jnp.bfloat16)
+                )
+
+        for index, (sends, _) in enumerate(PLAN):
+            for side, condition in sends:
+                @pl.when(both(has[side], flag_of(condition)))
+                def _(index=index, part=part, side=side):
+                    transfer(index, part, side).start()
 
     for index in range(len(NAMES)):
         acc[index] = jnp.zeros((basis, basis), jnp.float32)
@@ -159,22 +138,17 @@
         right = jnp.concatenate([blocks[second, o] for o in range(start, end)], axis=1)
         return row_dot(left, right)
 
-    load_half.wait()
-    load_coef.wait()
-
     dens_turned = dens_ref[...].astype(jnp.float32).T.astype(jnp.bfloat16)
-    lanes = stage.shape[2]
-    block = stage.shape[1] // basis
-
-    @pl.loop(0, basis // block)
+
+    @pl.loop(0, steps)
     def _(step):
-        @pl.loop(0, block)
-        def _(m):
+        for m in range(block):
             at = pl.multiple_of((step * block + m) * basis, basis)
             value = row_dot(dens_turned, coef[:, pl.ds(at, basis)])
-            to = pl.multiple_of(m * basis, basis)
             for part in range(stage.shape[0]):
-                stage[part, pl.ds(to, basis), :] = value[:, part * lanes:(part + 1) * lanes]
+                stage[part, m * basis:(m + 1) * basis, :] = (
+                    value[:, part * lanes:(part + 1) * lanes]
+                )
 
         first = pl.multiple_of(step * block, block)
 
@@ -232,7 +206,8 @@
 
             @pl.when(both(has[source], flag_of(condition)))
             def _(index=index, source=source):
-                arrival(index, source).wait_recv()
+                for part in range(parts):
+                    arrival(index, part, source).wait_recv()
 
         for first, second in products:
             there = has[second] if first == OWN else jnp.logical_and(has[first], has[second])
@@ -296,14 +271,12 @@
     swap_final = to_partner(final, aux_final, 1)
     swap_final.start()
 
-    self_scale, pair_scale, full_scale = scales
     swap_local.wait_recv()
-    self_ref[0, 0] = (local[0, ours, :] + aux_local[0]) * self_scale
-    full_ref[0, 0] = (local[1, ours, :] + aux_local[1]) * full_scale
+    out_ref[8] = local[0, ours, :] + aux_local[0]
+    out_ref[9] = local[1, ours, :] + aux_local[1]
     swap_final.wait_recv()
     for d in range(8):
-        factor = mask_ref[d].astype(jnp.float32)
-        pair_ref[0, 0, d] = (final[d, ours, :] + aux_final[d]) * pair_scale * factor
+        out_ref[d] = final[d, ours, :] + aux_final[d]
 
     swap_local.wait_send()
     swap_final.wait_send()
@@ -315,7 +288,17 @@
         for side, condition in sends:
             @pl.when(both(has[side], flag_of(condition)))
             def _(index=index, side=side):
-                transfer(index, side).wait_send()
+                for part in range(parts):
+                    transfer(index, part, side).wait_send()
+
+
+def finish_kernel(scales, sums_ref, mask_ref, self_ref, pair_ref, full_ref):
+    self_scale, pair_scale, full_scale = scales
+    for d in range(8):
+        factor = mask_ref[d].astype(jnp.float32)
+        pair_ref[0, 0, d] = sums_ref[d] * pair_scale * factor
+    self_ref[0, 0] = sums_ref[8] * self_scale
+    full_ref[0, 0] = sums_ref[9] * full_scale
 
 
 def local_step(rows, cols, aux, coef_three, orbitals, density, pair_mask):
@@ -326,26 +309,20 @@
     scales = (
         1.0 / (q_total * occ), 1.0 / (q_total * occ) ** 0.5, 1.0 / (q_total * basis) ** 0.5
     )
-    half = half_transform(coef, orbitals[0, 0])
     rows_out = basis // aux
     lanes = 128
     f32 = jnp.float32
     dma = pltpu.SemaphoreType.DMA
     vmem = pl.BlockSpec(memory_space=pltpu.VMEM)
-    return pl.pallas_call(
-        functools.partial(exchange_kernel, rows, cols, scales),
-        out_shape=(
-            jax.ShapeDtypeStruct((1, 1, rows_out, basis), f32),
-            jax.ShapeDtypeStruct((1, 1, 8, rows_out, basis), f32),
-            jax.ShapeDtypeStruct((1, 1, rows_out, basis), f32),
-        ),
+    sums = pl.pallas_call(
+        functools.partial(exchange_kernel, rows, cols),
+        out_shape=jax.ShapeDtypeStruct((10, rows_out, basis), f32),
         in_specs=[
             pl.BlockSpec(memory_space=pl.ANY),
-            pl.BlockSpec(memory_space=pl.ANY),
             vmem,
-            pl.BlockSpec(memory_space=pltpu.SMEM),
+            vmem,
         ],
-        out_specs=(vmem, vmem, vmem),
+        out_specs=vmem,
         scratch_shapes=[
             pltpu.VMEM((5, occ, basis, q_local), jnp.bfloat16),
             pltpu.VMEM((q_local, width), jnp.bfloat16),
@@ -358,9 +335,9 @@
             pltpu.VMEM((8, basis, basis), f32),
             pltpu.VMEM((2, rows_out, basis), f32),
             pltpu.VMEM((8, rows_out, basis), f32),
-            dma((2,)),
-            dma((4, len(PLAN))),
-            dma((4, len(PLAN))),
+            dma((q_local // lanes, basis // 16)),
+            dma((4, len(PLAN), q_local // lanes)),
+            dma((4, len(PLAN), q_local // lanes)),
             dma((4,)),
             dma((4,)),
             dma((2,)),
@@ -370,7 +347,18 @@
             collective_id=0, has_side_effects=True, vmem_limit_bytes=56 << 20
         ),
         name="exchange",
-    )(half, coef, density[0, 0], pair_mask[0, 0])
+    )(coef, orbitals[0, 0], density[0, 0])
+    return pl.pallas_call(
+        functools.partial(finish_kernel, scales),
+        out_shape=(
+            jax.ShapeDtypeStruct((1, 1, rows_out, basis), f32),
+            jax.ShapeDtypeStruct((1, 1, 8, rows_out, basis), f32),
+            jax.ShapeDtypeStruct((1, 1, rows_out, basis), f32),
+        ),
+        in_specs=[vmem, pl.BlockSpec(memory_space=pltpu.SMEM)],
+        out_specs=(vmem, vmem, vmem),
+        name="finish",
+    )(sums, pair_mask[0, 0])
 
 
 def solution(mesh):

time: 75.9 us -> 60.8 us (0.80)
  local copies, waits for them, and re-layouts: 9.99 us -> 0 us
  Pallas kernels: 64.8 us -> 59.9 us
    unnamed x9 -> x0, local copies, waits for them, and re-layouts: 9.99 us -> none
    pallas_call x2, Pallas kernels: 64.8 us -> 59.9 us  [the longest x1 58.2 us: local_step(): pl.pallas_call(functools.partial(exchange_kernel, rows, cols), out_shape=...]
where the time goes in v2:
time: 60.8 us; the launch traced here: 60.6 us
  Pallas kernels  59.9 us (99%)
  between operations  0.64 us (1%)
    pallas_call x1, Pallas kernels, local_step(): pl.pallas_call(functools.partial(exchange_kernel, rows, cols), out_shape=...  58.2 us
    pallas_call x1, Pallas kernels, local_step(): pl.pallas_call(functools.partial(finish_kernel, scales), out_shape=(jax.S...  1.72 us

profile of v2, /device:TPU:0, one launch (start us, length us, event | category | flops | bytes accessed | tf_op | source)
XLA Modules:
  0.0 60.6 jit_solution(2158094739115236710)
XLA Ops:
  0.6 58.2 %exchange.1.sums_ref = f32[10,64,128]{2,1,0:T(8,128)} custom-call(bf16[256,16384]{1,0:T(8,128)(2,1)} %bitcast.4, bf16[40,128]{1,0:T(8,128)(2,1)} %bitcast.6, bf16[128,128]{1,0:T(8,128)(2,1)} %bitcast.5), custom_call_target="tpu_custom_call" | custom-call | tf_op jit(solution)/shard_map/exchange/pallas_call | solution.py:317
  58.8 1.7 %finish.1 = (f32[1,1,64,128]{3,2,1,0:T(8,128)}, f32[1,1,8,64,128]{4,3,2,1,0:T(8,128)}, f32[1,1,64,128]{3,2,1,0:T(8,128)}) custom-call(f32[10,64,128]{2,1,0:T(8,128)} %exchange.1.sums_ref, s32[8]{0:T(128)} %bitcast.7), custom_call_target="tpu_custom_call" | custom-call | tf_op jit(solution)/shard_map/finish/pallas_call | solution.py:351
